TPU v7x, 256 devices: a whole 4x4x8 slice. The times are simulated.
256 devices in a mesh: panel: 8 (over z), rows: 32 (over y, x, core).
Axes of the slice: x: 4, y: 4, z: 8, core: 2. Of those that a mesh axis runs over, the one named last changes fastest.
Arguments:
- rhs_diag: bfloat16 [8, 8192, 128], P(None, 'rows'), may hold values from -6 to 6
- rhs_tall: bfloat16 [8, 16384, 128], P('panel', 'rows'), may hold values from -6 to 6
- diag_inverse: bfloat16 [8, 1024, 1024], P('panel'), may hold values from -0.1875 to 0.1875
- coupling: bfloat16 [8, 8192, 1024], P('panel', 'rows'), may hold values from -0.09375 to 0.09375
- tall_blocks: bfloat16 [8, 128, 128, 1024], P('panel', 'rows'), may hold values from -0.125 to 0.125
- sparsity: int32 [128, 8], P('rows', 'panel'), may hold values 0 or 1
Outputs:
- solution: float32 [8, 8, 1024, 128], P('panel', None, 'rows')
- tall_residual: float32 [8, 16384, 128], P('panel', 'rows')
All inputs are finite; a program needn't handle non-finite values. No bound on the sum of `sparsity` on one device may be relied on, other than what follows from the above.
Results may differ from a plain program's by a relative error of at most 0.0085.
Values may be sent and summed in bfloat16 or wider, within the bound.
No kernel may reach another device: no remote copies, remote signals or barrier semaphores. Data moves between devices by JAX's collectives and lax.ppermute only.
A program may use at most 64 MiB of HBM per device.

v0:
```python
import jax
import jax.numpy as jnp
from jax import lax
from jax.sharding import PartitionSpec as P


def shifted(block, axis, distance):
    devices = range(lax.axis_size(axis))
    route = [(i - distance, i) for i in devices if i - distance in devices]
    return lax.ppermute(block, axis, route)


def per_device(rhs_diag, rhs_tall, diag_inverse, coupling, tall_blocks, sparsity):
    panel_index = lax.axis_index("panel")
    rows_index = lax.axis_index("rows")
    panel_count = lax.axis_size("panel")
    rows_count = lax.axis_size("rows")
    batches, rows_here, columns = rhs_diag.shape
    panel_width = diag_inverse.shape[1]
    slice_rows = panel_width // rows_count
    blocks_here = tall_blocks.shape[1]
    block_rows = tall_blocks.shape[2]
    tall_rows = blocks_here * block_rows
    rows_panel = rows_index * rows_here // panel_width
    offset = jnp.clip(
        rows_index * rows_here - panel_index * panel_width, 0, panel_width - rows_here
    )
    inverse_cols = lax.dynamic_slice_in_dim(diag_inverse[0], offset, rows_here, 1)
    owner = rows_panel == panel_index
    is_later = rows_panel > panel_index
    coupling_here = coupling[0]
    tall_matrix = tall_blocks[0].reshape(tall_rows, panel_width)
    block_mask = jnp.repeat(sparsity[:, 0].astype(jnp.float32), block_rows)[:, None]

    def advance(tick_number, state_now):
        incoming, solutions, stored = state_now
        batch_now = tick_number - panel_index
        active = (batch_now >= 0) & (batch_now < batches)
        batch_safe = jnp.clip(batch_now, 0, batches - 1)
        rhs_now = lax.dynamic_index_in_dim(rhs_diag, batch_safe, 0, keepdims=False).astype(
            jnp.float32
        )
        reduced = (rhs_now - incoming).astype(jnp.bfloat16)
        partial_value = jnp.dot(inverse_cols, reduced, preferred_element_type=jnp.float32)
        partial_value = jnp.where(owner, partial_value, jnp.float32(0.0))
        summed_all = lax.psum(partial_value, "rows")
        own_rows = lax.dynamic_slice_in_dim(summed_all, rows_index * slice_rows, slice_rows, 0)
        solved = summed_all.astype(jnp.bfloat16)
        previous = lax.dynamic_index_in_dim(solutions, batch_safe, 0, keepdims=False)
        solutions = lax.dynamic_update_index_in_dim(
            solutions, jnp.where(active, own_rows, previous), batch_safe, 0
        )
        update = jnp.dot(coupling_here, solved, preferred_element_type=jnp.float32)
        outgoing = incoming + jnp.where(is_later, update, jnp.float32(0.0))
        earlier = lax.dynamic_index_in_dim(stored, batch_safe, 0, keepdims=False)
        stored = lax.dynamic_update_index_in_dim(
            stored, jnp.where(active, solved, earlier), batch_safe, 0
        )
        incoming = shifted(outgoing, "panel", 1)
        return (incoming, solutions, stored)

    stored = jnp.zeros((batches, panel_width, columns), jnp.bfloat16)
    initial = (
        jnp.zeros((rows_here, columns), jnp.float32),
        jnp.zeros((batches, slice_rows, columns), jnp.float32),
        stored,
    )
    tick_count = batches + panel_count - 1
    incoming, solutions, stored = lax.fori_loop(0, tick_count, advance, initial)
    tall_terms = (
        jnp.einsum("rw,bws->brs", tall_matrix, stored, preferred_element_type=jnp.float32)
        * block_mask
    )
    summed = lax.psum_scatter(tall_terms, "panel", scatter_dimension=0, tiled=True)
    tall_residual = rhs_tall.astype(jnp.float32) - summed
    return (solutions[None], tall_residual)


def solution(mesh):
    placed = (
        P(None, "rows", None),
        P("panel", "rows", None),
        P("panel", None, None),
        P("panel", "rows", None),
        P("panel", "rows", None, None),
        P("rows", "panel"),
    )
    return jax.shard_map(
        per_device,
        mesh=mesh,
        in_specs=placed,
        out_specs=(P("panel", None, "rows", None), P("panel", "rows", None)),
        check_vma=False,
    )
```

profile of v0, /device:TPU:2, one launch (start us, length us, event | category | flops | bytes accessed | tf_op | source)
XLA Modules:
  0.0 1989.9 jit_solution(4910491097746578890)
XLA Ops:
  12.2 1919.9 %while.19 = (s32[]{:T(128)}, f32[256,128]{0,1:T(8,128)S(1)}, f32[8,32,128]{2,1,0:T(8,128)}, bf16[8,1024,128]{1,2,0:T(8,128)(2,1)}, pred[]{:T(512)}, /*index=5*/p...) while((s32[]{:T(128)}, f32[256,128]{0,1:T(8,128)S(1)}, ...), condition=%wide.region_2.3_spmd, body=%wide.region_0.2_spmd.sunk | while | flops 135041024 | bytes 8307022 | solution.py:69
  16.7 115.6 %all-reduce.2.cloned.1.call-done = f32[1024,128]{0,1:T(8,128)} async-done(((f32[1024,128]{0,1:T(8,128)}), f32[1024,128]{0,1:T(8,128)}) %all-reduce.2.cloned.1.call-update) | async-done | bytes 524304 | tf_op jit(solution)/shard_map/while/body/eval_jaxpr/psum | solution.py:46
  145.8 114.6 %all-reduce.2.cloned.1.call-done = f32[1024,128]{0,1:T(8,128)} async-done(((f32[1024,128]{0,1:T(8,128)}), f32[1024,128]{0,1:T(8,128)}) %all-reduce.2.cloned.1.call-update) | async-done | bytes 524304 | tf_op jit(solution)/shard_map/while/body/eval_jaxpr/psum | solution.py:46
  273.9 114.6 %all-reduce.2.cloned.1.call-done = f32[1024,128]{0,1:T(8,128)} async-done(((f32[1024,128]{0,1:T(8,128)}), f32[1024,128]{0,1:T(8,128)}) %all-reduce.2.cloned.1.call-update) | async-done | bytes 524304 | tf_op jit(solution)/shard_map/while/body/eval_jaxpr/psum | solution.py:46
  401.9 114.3 %all-reduce.2.cloned.1.call-done = f32[1024,128]{0,1:T(8,128)} async-done(((f32[1024,128]{0,1:T(8,128)}), f32[1024,128]{0,1:T(8,128)}) %all-reduce.2.cloned.1.call-update) | async-done | bytes 524304 | tf_op jit(solution)/shard_map/while/body/eval_jaxpr/psum | solution.py:46
  529.7 114.3 %all-reduce.2.cloned.1.call-done = f32[1024,128]{0,1:T(8,128)} async-done(((f32[1024,128]{0,1:T(8,128)}), f32[1024,128]{0,1:T(8,128)}) %all-reduce.2.cloned.1.call-update) | async-done | bytes 524304 | tf_op jit(solution)/shard_map/while/body/eval_jaxpr/psum | solution.py:46
  646.0 3.5 collective-permute-start
  657.5 114.2 %all-reduce.2.cloned.1.call-done = f32[1024,128]{0,1:T(8,128)} async-done(((f32[1024,128]{0,1:T(8,128)}), f32[1024,128]{0,1:T(8,128)}) %all-reduce.2.cloned.1.call-update) | async-done | bytes 524304 | tf_op jit(solution)/shard_map/while/body/eval_jaxpr/psum | solution.py:46
  785.2 114.6 %all-reduce.2.cloned.1.call-done = f32[1024,128]{0,1:T(8,128)} async-done(((f32[1024,128]{0,1:T(8,128)}), f32[1024,128]{0,1:T(8,128)}) %all-reduce.2.cloned.1.call-update) | async-done | bytes 524304 | tf_op jit(solution)/shard_map/while/body/eval_jaxpr/psum | solution.py:46
  901.8 3.5 collective-permute-start
  913.2 114.6 %all-reduce.2.cloned.1.call-done = f32[1024,128]{0,1:T(8,128)} async-done(((f32[1024,128]{0,1:T(8,128)}), f32[1024,128]{0,1:T(8,128)}) %all-reduce.2.cloned.1.call-update) | async-done | bytes 524304 | tf_op jit(solution)/shard_map/while/body/eval_jaxpr/psum | solution.py:46
  1041.3 114.6 %all-reduce.2.cloned.1.call-done = f32[1024,128]{0,1:T(8,128)} async-done(((f32[1024,128]{0,1:T(8,128)}), f32[1024,128]{0,1:T(8,128)}) %all-reduce.2.cloned.1.call-update) | async-done | bytes 524304 | tf_op jit(solution)/shard_map/while/body/eval_jaxpr/psum | solution.py:46
  1169.4 114.3 %all-reduce.2.cloned.1.call-done = f32[1024,128]{0,1:T(8,128)} async-done(((f32[1024,128]{0,1:T(8,128)}), f32[1024,128]{0,1:T(8,128)}) %all-reduce.2.cloned.1.call-update) | async-done | bytes 524304 | tf_op jit(solution)/shard_map/while/body/eval_jaxpr/psum | solution.py:46
  1285.7 3.5 collective-permute-start
  1297.1 114.6 %all-reduce.2.cloned.1.call-done = f32[1024,128]{0,1:T(8,128)} async-done(((f32[1024,128]{0,1:T(8,128)}), f32[1024,128]{0,1:T(8,128)}) %all-reduce.2.cloned.1.call-update) | async-done | bytes 524304 | tf_op jit(solution)/shard_map/while/body/eval_jaxpr/psum | solution.py:46
  1413.8 3.5 collective-permute-start
  1425.2 114.3 %all-reduce.2.cloned.1.call-done = f32[1024,128]{0,1:T(8,128)} async-done(((f32[1024,128]{0,1:T(8,128)}), f32[1024,128]{0,1:T(8,128)}) %all-reduce.2.cloned.1.call-update) | async-done | bytes 524304 | tf_op jit(solution)/shard_map/while/body/eval_jaxpr/psum | solution.py:46
  1541.6 3.5 collective-permute-start
  1553.0 114.6 %all-reduce.2.cloned.1.call-done = f32[1024,128]{0,1:T(8,128)} async-done(((f32[1024,128]{0,1:T(8,128)}), f32[1024,128]{0,1:T(8,128)}) %all-reduce.2.cloned.1.call-update) | async-done | bytes 524304 | tf_op jit(solution)/shard_map/while/body/eval_jaxpr/psum | solution.py:46
  1669.6 3.5 collective-permute-start
  1681.0 114.2 %all-reduce.2.cloned.1.call-done = f32[1024,128]{0,1:T(8,128)} async-done(((f32[1024,128]{0,1:T(8,128)}), f32[1024,128]{0,1:T(8,128)}) %all-reduce.2.cloned.1.call-update) | async-done | bytes 524304 | tf_op jit(solution)/shard_map/while/body/eval_jaxpr/psum | solution.py:46
  1808.8 114.3 %all-reduce.2.cloned.1.call-done = f32[1024,128]{0,1:T(8,128)} async-done(((f32[1024,128]{0,1:T(8,128)}), f32[1024,128]{0,1:T(8,128)}) %all-reduce.2.cloned.1.call-update) | async-done | bytes 524304 | tf_op jit(solution)/shard_map/while/body/eval_jaxpr/psum | solution.py:46
  1932.0 4.5 multiply_bitcast_fusion
  1937.5 43.4 %reduce-scatter.2.cloned.1.call-done = f32[1,512,128]{1,2,0:T(8,128)} async-done(((f32[8,512,128]{1,2,0:T(8,128)}), f32[1,512,128]{1,2,0:T(8,128)}) %reduce-scatter.2.cloned.1.call-update) | async-done | bytes 262160 | tf_op jit(solution)/shard_map/reduce_scatter | solution.py:74
  (266 shorter events, 187.8 us)
Async XLA Ops:
  12.2 120.1 %all-reduce.2.cloned.1.call-start = ((), (), s32[]{:S(2)}) async-start(), calls=%async_computation.2 | async-start | bytes 1048576 | tf_op jit(solution)/shard_map/while/body/eval_jaxpr/psum | solution.py:46
  141.2 119.2 %all-reduce.2.cloned.1.call-start = ((), (), s32[]{:S(2)}) async-start(), calls=%async_computation.2 | async-start | bytes 1048576 | tf_op jit(solution)/shard_map/while/body/eval_jaxpr/psum | solution.py:46
  269.3 119.1 %all-reduce.2.cloned.1.call-start = ((), (), s32[]{:S(2)}) async-start(), calls=%async_computation.2 | async-start | bytes 1048576 | tf_op jit(solution)/shard_map/while/body/eval_jaxpr/psum | solution.py:46
  397.4 118.8 %all-reduce.2.cloned.1.call-start = ((), (), s32[]{:S(2)}) async-start(), calls=%async_computation.2 | async-start | bytes 1048576 | tf_op jit(solution)/shard_map/while/body/eval_jaxpr/psum | solution.py:46
  525.1 118.8 %all-reduce.2.cloned.1.call-start = ((), (), s32[]{:S(2)}) async-start(), calls=%async_computation.2 | async-start | bytes 1048576 | tf_op jit(solution)/shard_map/while/body/eval_jaxpr/psum | solution.py:46
  646.0 6.9 collective-permute-start
  652.9 118.8 %all-reduce.2.cloned.1.call-start = ((), (), s32[]{:S(2)}) async-start(), calls=%async_computation.2 | async-start | bytes 1048576 | tf_op jit(solution)/shard_map/while/body/eval_jaxpr/psum | solution.py:46
  780.6 119.1 %all-reduce.2.cloned.1.call-start = ((), (), s32[]{:S(2)}) async-start(), calls=%async_computation.2 | async-start | bytes 1048576 | tf_op jit(solution)/shard_map/while/body/eval_jaxpr/psum | solution.py:46
  908.7 119.1 %all-reduce.2.cloned.1.call-start = ((), (), s32[]{:S(2)}) async-start(), calls=%async_computation.2 | async-start | bytes 1048576 | tf_op jit(solution)/shard_map/while/body/eval_jaxpr/psum | solution.py:46
  1029.8 6.9 collective-permute-start
  1036.7 119.1 %all-reduce.2.cloned.1.call-start = ((), (), s32[]{:S(2)}) async-start(), calls=%async_computation.2 | async-start | bytes 1048576 | tf_op jit(solution)/shard_map/while/body/eval_jaxpr/psum | solution.py:46
  1157.9 6.9 collective-permute-start
  1164.8 118.8 %all-reduce.2.cloned.1.call-start = ((), (), s32[]{:S(2)}) async-start(), calls=%async_computation.2 | async-start | bytes 1048576 | tf_op jit(solution)/shard_map/while/body/eval_jaxpr/psum | solution.py:46
  1285.7 6.9 collective-permute-start
  1292.6 119.1 %all-reduce.2.cloned.1.call-start = ((), (), s32[]{:S(2)}) async-start(), calls=%async_computation.2 | async-start | bytes 1048576 | tf_op jit(solution)/shard_map/while/body/eval_jaxpr/psum | solution.py:46
  1413.8 6.9 collective-permute-start
  1420.7 118.8 %all-reduce.2.cloned.1.call-start = ((), (), s32[]{:S(2)}) async-start(), calls=%async_computation.2 | async-start | bytes 1048576 | tf_op jit(solution)/shard_map/while/body/eval_jaxpr/psum | solution.py:46
  1541.6 6.9 collective-permute-start
  1548.5 119.1 %all-reduce.2.cloned.1.call-start = ((), (), s32[]{:S(2)}) async-start(), calls=%async_computation.2 | async-start | bytes 1048576 | tf_op jit(solution)/shard_map/while/body/eval_jaxpr/psum | solution.py:46
  1669.6 6.9 collective-permute-start
  1676.5 118.8 %all-reduce.2.cloned.1.call-start = ((), (), s32[]{:S(2)}) async-start(), calls=%async_computation.2 | async-start | bytes 1048576 | tf_op jit(solution)/shard_map/while/body/eval_jaxpr/psum | solution.py:46
  1804.2 118.8 %all-reduce.2.cloned.1.call-start = ((), (), s32[]{:S(2)}) async-start(), calls=%async_computation.2 | async-start | bytes 1048576 | tf_op jit(solution)/shard_map/while/body/eval_jaxpr/psum | solution.py:46
  1925.1 6.9 collective-permute-start
  1932.0 48.9 %reduce-scatter.2.cloned.1.call-start = ((), (), s32[]{:S(2)}) async-start(), calls=%async_computation.1 | async-start | bytes 2359296 | tf_op jit(solution)/shard_map/reduce_scatter | solution.py:74
  (25 other events, 164.8 us)
Sparse Core Ops, SparseCore 0:
  16.2 116.0 all-reduce.1
  145.2 115.0 all-reduce.1
  273.3 115.0 all-reduce.1
  401.1 115.0 all-reduce.1
  528.8 115.0 all-reduce.1
  656.6 115.0 all-reduce.1
  784.6 115.0 all-reduce.1
  912.7 115.0 all-reduce.1
  1040.8 115.0 all-reduce.1
  1168.5 115.0 all-reduce.1
  1296.6 115.0 all-reduce.1
  1424.4 115.0 all-reduce.1
  1552.5 115.0 all-reduce.1
  1680.2 115.0 all-reduce.1
  1807.9 115.0 all-reduce.1
Sparse Core Ops, SparseCore 1:
  1936.6 44.3 reduce-scatter.1
where the time goes:
time: 1990 us
  waiting for transfers between devices  1760 us (88%)
  local copies, waits for them, and re-layouts  66.1 us (3%)
  matrix products  51.9 us (3%)
  starting transfers between devices  51.8 us (3%)
  other arithmetic  42.9 us (2%)
    psum x15, waiting for transfers between devices, advance(): summed_all = lax.psum(partial_value, 'rows')  1720 us
    ppermute x15, starting transfers between devices, shifted(): return lax.ppermute(block, axis, route)  51.8 us
    reduce_scatter x1, waiting for transfers between devices, per_device(): lax.psum_scatter(tall_terms, 'panel', scatter_dimension=0, tiled=True)  43.4 us
  transfers between devices with their start and end apart: 31, of which 16 were waited for; matrix products, arithmetic and copies ran while one was open for 4% of the time, Pallas kernels for 0%

commit v1 on v0

--- a/solution.py
+++ b/solution.py
@@ -43,7 +43,25 @@
         reduced = (rhs_now - incoming).astype(jnp.bfloat16)
         partial_value = jnp.dot(inverse_cols, reduced, preferred_element_type=jnp.float32)
         partial_value = jnp.where(owner, partial_value, jnp.float32(0.0))
-        summed_all = lax.psum(partial_value, "rows")
+
+        def recover_tasks_in(field_in):
+            q_n = lax.axis_size("rows")
+
+            def _write_rings(part_next, kept_arr):
+                if kept_arr >= q_n:
+                    return part_next
+                pile = []
+                for q in tuple(range(q_n)):
+                    pile.append((q, q ^ kept_arr))
+                item_now = _write_rings(
+                    part_next + lax.ppermute(part_next, "rows", pile), 2 * kept_arr
+                )
+                return item_now
+
+            raw_out = _write_rings(field_in, 1)
+            return raw_out
+
+        summed_all = recover_tasks_in(partial_value)
         own_rows = lax.dynamic_slice_in_dim(summed_all, rows_index * slice_rows, slice_rows, 0)
         solved = summed_all.astype(jnp.bfloat16)
         previous = lax.dynamic_index_in_dim(solutions, batch_safe, 0, keepdims=False)

time: 1990 us -> 1090 us (0.55)
  waiting for transfers between devices: 1760 us -> 813 us
  starting transfers between devices: 51.8 us -> 174 us
  matrix products: 51.9 us -> 13.7 us
  local copies, waits for them, and re-layouts: 66.1 us -> 36.6 us
    psum x15 -> x0, waiting for transfers between devices: 1720 us -> none  [advance(): summed_all = lax.psum(partial_value, 'rows')]
    ppermute x0 -> x75, waiting for transfers between devices: none -> 728 us  [_write_rings(): lax.ppermute(part_next, 'rows', pile)]
    ppermute x0 -> x75, starting transfers between devices: none -> 96.9 us  [_write_rings(): lax.ppermute(part_next, 'rows', pile)]
    ppermute x15, waiting for transfers between devices: 0.04 us -> 35 us  [shifted(): return lax.ppermute(block, axis, route)]
    dot_general x15, matrix products: 30.6 us -> 4.65 us  [advance(): update = jnp.dot(coupling_here, solved, preferred_element_type=jnp.float32)]
    ppermute x15, starting transfers between devices: 51.8 us -> 77 us  [shifted(): return lax.ppermute(block, axis, route)]
    dynamic_slice x30, local copies, waits for them, and re-layouts: 21.8 us -> 1.52 us  [advance(): lax.dynamic_index_in_dim(solutions, batch_safe, 0, keepdims=False)]
  transfers between devices with their start and end apart: 31 -> 91, of which waited for: 16 -> 91; matrix products, arithmetic and copies ran while one was open for 4% -> 2% of each run, Pallas kernels for 0% -> 0%
where the time goes in v1:
time: 1090 us
  waiting for transfers between devices  813 us (75%)
  starting transfers between devices  174 us (16%)
  local copies, waits for them, and re-layouts  36.6 us (3%)
  other arithmetic  34.4 us (3%)
  between operations  14.1 us (1%)
  matrix products  13.7 us (1%)
    ppermute x75, waiting for transfers between devices, _write_rings(): lax.ppermute(part_next, 'rows', pile)  728 us
    ppermute x75, starting transfers between devices, _write_rings(): lax.ppermute(part_next, 'rows', pile)  96.9 us
    ppermute x15, starting transfers between devices, shifted(): return lax.ppermute(block, axis, route)  77 us
    reduce_scatter x1, waiting for transfers between devices, per_device(): lax.psum_scatter(tall_terms, 'panel', scatter_dimension=0, tiled=True)  49.3 us
    ppermute x15, waiting for transfers between devices, shifted(): return lax.ppermute(block, axis, route)  35 us
    dynamic_update_slice x15, other arithmetic, advance(): lax.dynamic_update_index_in_dim(stored, jnp.where(active, solved, earlier...  27.8 us
  transfers between devices with their start and end apart: 91, of which 91 were waited for; matrix products, arithmetic and copies ran while one was open for 2% of the time, Pallas kernels for 0%

profile of v1, /device:TPU:2, one launch (start us, length us, event | category | flops | bytes accessed | tf_op | source)
XLA Modules:
  0.0 1086.9 jit_solution(10306877320786490651)
XLA Ops:
  10.6 1012.8 %while.19 = (s32[]{:T(128)}, f32[256,128]{0,1:T(8,128)S(1)}, f32[8,32,128]{2,1,0:T(8,128)S(1)}, bf16[8,1024,128]{1,2,0:T(8,128)(2,1)}, pred[]{:T(512)}, /*index=...) while((s32[]{:T(128)}, f32[256,128]{0,1:T(8,128)S(1)}, ...), condition=%wide.region_1.2_spmd, body=%wide.region_0.1_spmd.sunk | while | flops 135565312 | bytes 25018860 | solution.py:87
  30.3 13.4 %collective-permute-done.2 = f32[1024,128]{0,1:T(8,128)S(1)} collective-permute-done((f32[1024,128]{0,1:T(8,128)S(1)}, f32[1024,128]{0,1:T(8,128)S(1)}, u32[]{:S(2)}, u32[]{:S(2)}) %collective-permute-start.2) | collective-permute-done | bytes 524320 | tf_op jit(solution)/shard_map/while/body/eval_jaxpr/ppermute | solution.py:57
  81.4 13.4 %collective-permute-done.1 = f32[1024,128]{0,1:T(8,128)S(1)} collective-permute-done((f32[1024,128]{0,1:T(8,128)S(1)}, f32[1024,128]{0,1:T(8,128)S(1)}, u32[]{:S(2)}, u32[]{:S(2)}) %collective-permute-start.1) | collective-permute-done | bytes 524320 | tf_op jit(solution)/shard_map/while/body/eval_jaxpr/ppermute | solution.py:57
  97.2 12.5 %collective-permute-done.2 = f32[1024,128]{0,1:T(8,128)S(1)} collective-permute-done((f32[1024,128]{0,1:T(8,128)S(1)}, f32[1024,128]{0,1:T(8,128)S(1)}, u32[]{:S(2)}, u32[]{:S(2)}) %collective-permute-start.2) | collective-permute-done | bytes 524320 | tf_op jit(solution)/shard_map/while/body/eval_jaxpr/ppermute | solution.py:57
  148.1 13.4 %collective-permute-done.1 = f32[1024,128]{0,1:T(8,128)S(1)} collective-permute-done((f32[1024,128]{0,1:T(8,128)S(1)}, f32[1024,128]{0,1:T(8,128)S(1)}, u32[]{:S(2)}, u32[]{:S(2)}) %collective-permute-start.1) | collective-permute-done | bytes 524320 | tf_op jit(solution)/shard_map/while/body/eval_jaxpr/ppermute | solution.py:57
  163.8 12.5 %collective-permute-done.2 = f32[1024,128]{0,1:T(8,128)S(1)} collective-permute-done((f32[1024,128]{0,1:T(8,128)S(1)}, f32[1024,128]{0,1:T(8,128)S(1)}, u32[]{:S(2)}, u32[]{:S(2)}) %collective-permute-start.2) | collective-permute-done | bytes 524320 | tf_op jit(solution)/shard_map/while/body/eval_jaxpr/ppermute | solution.py:57
  214.7 13.4 %collective-permute-done.1 = f32[1024,128]{0,1:T(8,128)S(1)} collective-permute-done((f32[1024,128]{0,1:T(8,128)S(1)}, f32[1024,128]{0,1:T(8,128)S(1)}, u32[]{:S(2)}, u32[]{:S(2)}) %collective-permute-start.1) | collective-permute-done | bytes 524320 | tf_op jit(solution)/shard_map/while/body/eval_jaxpr/ppermute | solution.py:57
  230.4 12.5 %collective-permute-done.2 = f32[1024,128]{0,1:T(8,128)S(1)} collective-permute-done((f32[1024,128]{0,1:T(8,128)S(1)}, f32[1024,128]{0,1:T(8,128)S(1)}, u32[]{:S(2)}, u32[]{:S(2)}) %collective-permute-start.2) | collective-permute-done | bytes 524320 | tf_op jit(solution)/shard_map/while/body/eval_jaxpr/ppermute | solution.py:57
  281.4 13.4 %collective-permute-done.1 = f32[1024,128]{0,1:T(8,128)S(1)} collective-permute-done((f32[1024,128]{0,1:T(8,128)S(1)}, f32[1024,128]{0,1:T(8,128)S(1)}, u32[]{:S(2)}, u32[]{:S(2)}) %collective-permute-start.1) | collective-permute-done | bytes 524320 | tf_op jit(solution)/shard_map/while/body/eval_jaxpr/ppermute | solution.py:57
  297.1 12.5 %collective-permute-done.2 = f32[1024,128]{0,1:T(8,128)S(1)} collective-permute-done((f32[1024,128]{0,1:T(8,128)S(1)}, f32[1024,128]{0,1:T(8,128)S(1)}, u32[]{:S(2)}, u32[]{:S(2)}) %collective-permute-start.2) | collective-permute-done | bytes 524320 | tf_op jit(solution)/shard_map/while/body/eval_jaxpr/ppermute | solution.py:57
  348.9 13.4 %collective-permute-done.1 = f32[1024,128]{0,1:T(8,128)S(1)} collective-permute-done((f32[1024,128]{0,1:T(8,128)S(1)}, f32[1024,128]{0,1:T(8,128)S(1)}, u32[]{:S(2)}, u32[]{:S(2)}) %collective-permute-start.1) | collective-permute-done | bytes 524320 | tf_op jit(solution)/shard_map/while/body/eval_jaxpr/ppermute | solution.py:57
  364.6 12.5 %collective-permute-done.2 = f32[1024,128]{0,1:T(8,128)S(1)} collective-permute-done((f32[1024,128]{0,1:T(8,128)S(1)}, f32[1024,128]{0,1:T(8,128)S(1)}, u32[]{:S(2)}, u32[]{:S(2)}) %collective-permute-start.2) | collective-permute-done | bytes 524320 | tf_op jit(solution)/shard_map/while/body/eval_jaxpr/ppermute | solution.py:57
  416.7 13.4 %collective-permute-done.1 = f32[1024,128]{0,1:T(8,128)S(1)} collective-permute-done((f32[1024,128]{0,1:T(8,128)S(1)}, f32[1024,128]{0,1:T(8,128)S(1)}, u32[]{:S(2)}, u32[]{:S(2)}) %collective-permute-start.1) | collective-permute-done | bytes 524320 | tf_op jit(solution)/shard_map/while/body/eval_jaxpr/ppermute | solution.py:57
  484.6 13.4 %collective-permute-done.1 = f32[1024,128]{0,1:T(8,128)S(1)} collective-permute-done((f32[1024,128]{0,1:T(8,128)S(1)}, f32[1024,128]{0,1:T(8,128)S(1)}, u32[]{:S(2)}, u32[]{:S(2)}) %collective-permute-start.1) | collective-permute-done | bytes 524320 | tf_op jit(solution)/shard_map/while/body/eval_jaxpr/ppermute | solution.py:57
  500.3 12.5 %collective-permute-done.2 = f32[1024,128]{0,1:T(8,128)S(1)} collective-permute-done((f32[1024,128]{0,1:T(8,128)S(1)}, f32[1024,128]{0,1:T(8,128)S(1)}, u32[]{:S(2)}, u32[]{:S(2)}) %collective-permute-start.2) | collective-permute-done | bytes 524320 | tf_op jit(solution)/shard_map/while/body/eval_jaxpr/ppermute | solution.py:57
  552.4 13.4 %collective-permute-done.1 = f32[1024,128]{0,1:T(8,128)S(1)} collective-permute-done((f32[1024,128]{0,1:T(8,128)S(1)}, f32[1024,128]{0,1:T(8,128)S(1)}, u32[]{:S(2)}, u32[]{:S(2)}) %collective-permute-start.1) | collective-permute-done | bytes 524320 | tf_op jit(solution)/shard_map/while/body/eval_jaxpr/ppermute | solution.py:57
  568.1 12.5 %collective-permute-done.2 = f32[1024,128]{0,1:T(8,128)S(1)} collective-permute-done((f32[1024,128]{0,1:T(8,128)S(1)}, f32[1024,128]{0,1:T(8,128)S(1)}, u32[]{:S(2)}, u32[]{:S(2)}) %collective-permute-start.2) | collective-permute-done | bytes 524320 | tf_op jit(solution)/shard_map/while/body/eval_jaxpr/ppermute | solution.py:57
  620.3 13.4 %collective-permute-done.1 = f32[1024,128]{0,1:T(8,128)S(1)} collective-permute-done((f32[1024,128]{0,1:T(8,128)S(1)}, f32[1024,128]{0,1:T(8,128)S(1)}, u32[]{:S(2)}, u32[]{:S(2)}) %collective-permute-start.1) | collective-permute-done | bytes 524320 | tf_op jit(solution)/shard_map/while/body/eval_jaxpr/ppermute | solution.py:57
  688.1 13.4 %collective-permute-done.1 = f32[1024,128]{0,1:T(8,128)S(1)} collective-permute-done((f32[1024,128]{0,1:T(8,128)S(1)}, f32[1024,128]{0,1:T(8,128)S(1)}, u32[]{:S(2)}, u32[]{:S(2)}) %collective-permute-start.1) | collective-permute-done | bytes 524320 | tf_op jit(solution)/shard_map/while/body/eval_jaxpr/ppermute | solution.py:57
  756.0 13.4 %collective-permute-done.1 = f32[1024,128]{0,1:T(8,128)S(1)} collective-permute-done((f32[1024,128]{0,1:T(8,128)S(1)}, f32[1024,128]{0,1:T(8,128)S(1)}, u32[]{:S(2)}, u32[]{:S(2)}) %collective-permute-start.1) | collective-permute-done | bytes 524320 | tf_op jit(solution)/shard_map/while/body/eval_jaxpr/ppermute | solution.py:57
  823.8 13.4 %collective-permute-done.1 = f32[1024,128]{0,1:T(8,128)S(1)} collective-permute-done((f32[1024,128]{0,1:T(8,128)S(1)}, f32[1024,128]{0,1:T(8,128)S(1)}, u32[]{:S(2)}, u32[]{:S(2)}) %collective-permute-start.1) | collective-permute-done | bytes 524320 | tf_op jit(solution)/shard_map/while/body/eval_jaxpr/ppermute | solution.py:57
  891.7 13.4 %collective-permute-done.1 = f32[1024,128]{0,1:T(8,128)S(1)} collective-permute-done((f32[1024,128]{0,1:T(8,128)S(1)}, f32[1024,128]{0,1:T(8,128)S(1)}, u32[]{:S(2)}, u32[]{:S(2)}) %collective-permute-start.1) | collective-permute-done | bytes 524320 | tf_op jit(solution)/shard_map/while/body/eval_jaxpr/ppermute | solution.py:57
  959.6 13.4 %collective-permute-done.1 = f32[1024,128]{0,1:T(8,128)S(1)} collective-permute-done((f32[1024,128]{0,1:T(8,128)S(1)}, f32[1024,128]{0,1:T(8,128)S(1)}, u32[]{:S(2)}, u32[]{:S(2)}) %collective-permute-start.1) | collective-permute-done | bytes 524320 | tf_op jit(solution)/shard_map/while/body/eval_jaxpr/ppermute | solution.py:57
  1029.0 49.3 %reduce-scatter.2.cloned.1.call-done = f32[1,512,128]{1,2,0:T(8,128)} async-done(((f32[8,512,128]{1,2,0:T(8,128)}), f32[1,512,128]{1,2,0:T(8,128)}) %reduce-scatter.2.cloned.1.call-update) | async-done | bytes 262160 | tf_op jit(solution)/shard_map/reduce_scatter | solution.py:92
  (431 shorter events, 733.2 us)
Async XLA Ops:
  7.2 1071.1 %reduce-scatter.2.cloned.1.call-start = ((), (), s32[]{:S(2)}) async-start(), calls=%async_computation.1 | async-start | bytes 2359296 | tf_op jit(solution)/shard_map/reduce_scatter | solution.py:92
  14.0 14.6 %collective-permute-start.1 = (f32[1024,128]{0,1:T(8,128)S(1)}, f32[1024,128]{0,1:T(8,128)S(1)}, u32[]{:S(2)}, u32[]{:S(2)}) collective-permute-start(f32[1024,128]{0,1:T(8,128)S(1)} %add.111), channel_id=1, source_target_pairs={{0,2},{1,3},{2,0},{3,1},{4,6},{5,7},{6,4},{7,5},{8,10},{9,11},{10,... | collective-permute-start | bytes 1572872 | tf_op jit(solution)/shard_map/while/body/eval_jaxpr/ppermute | solution.py:57
  28.6 15.0 %collective-permute-start.2 = (f32[1024,128]{0,1:T(8,128)S(1)}, f32[1024,128]{0,1:T(8,128)S(1)}, u32[]{:S(2)}, u32[]{:S(2)}) collective-permute-start(f32[1024,128]{0,1:T(8,128)S(1)} %add.112), channel_id=1, source_target_pairs={{0,4},{1,5},{2,6},{3,7},{4,0},{5,1},{6,2},{7,3},{8,12},{9,13},{10,... | collective-permute-start | bytes 1572872 | tf_op jit(solution)/shard_map/while/body/eval_jaxpr/ppermute | solution.py:57
  80.8 14.1 %collective-permute-start.1 = (f32[1024,128]{0,1:T(8,128)S(1)}, f32[1024,128]{0,1:T(8,128)S(1)}, u32[]{:S(2)}, u32[]{:S(2)}) collective-permute-start(f32[1024,128]{0,1:T(8,128)S(1)} %add.111), channel_id=1, source_target_pairs={{0,2},{1,3},{2,0},{3,1},{4,6},{5,7},{6,4},{7,5},{8,10},{9,11},{10,... | collective-permute-start | bytes 1572872 | tf_op jit(solution)/shard_map/while/body/eval_jaxpr/ppermute | solution.py:57
  94.9 14.7 %collective-permute-start.2 = (f32[1024,128]{0,1:T(8,128)S(1)}, f32[1024,128]{0,1:T(8,128)S(1)}, u32[]{:S(2)}, u32[]{:S(2)}) collective-permute-start(f32[1024,128]{0,1:T(8,128)S(1)} %add.112), channel_id=1, source_target_pairs={{0,4},{1,5},{2,6},{3,7},{4,0},{5,1},{6,2},{7,3},{8,12},{9,13},{10,... | collective-permute-start | bytes 1572872 | tf_op jit(solution)/shard_map/while/body/eval_jaxpr/ppermute | solution.py:57
  147.4 14.1 %collective-permute-start.1 = (f32[1024,128]{0,1:T(8,128)S(1)}, f32[1024,128]{0,1:T(8,128)S(1)}, u32[]{:S(2)}, u32[]{:S(2)}) collective-permute-start(f32[1024,128]{0,1:T(8,128)S(1)} %add.111), channel_id=1, source_target_pairs={{0,2},{1,3},{2,0},{3,1},{4,6},{5,7},{6,4},{7,5},{8,10},{9,11},{10,... | collective-permute-start | bytes 1572872 | tf_op jit(solution)/shard_map/while/body/eval_jaxpr/ppermute | solution.py:57
  161.6 14.7 %collective-permute-start.2 = (f32[1024,128]{0,1:T(8,128)S(1)}, f32[1024,128]{0,1:T(8,128)S(1)}, u32[]{:S(2)}, u32[]{:S(2)}) collective-permute-start(f32[1024,128]{0,1:T(8,128)S(1)} %add.112), channel_id=1, source_target_pairs={{0,4},{1,5},{2,6},{3,7},{4,0},{5,1},{6,2},{7,3},{8,12},{9,13},{10,... | collective-permute-start | bytes 1572872 | tf_op jit(solution)/shard_map/while/body/eval_jaxpr/ppermute | solution.py:57
  214.1 14.1 %collective-permute-start.1 = (f32[1024,128]{0,1:T(8,128)S(1)}, f32[1024,128]{0,1:T(8,128)S(1)}, u32[]{:S(2)}, u32[]{:S(2)}) collective-permute-start(f32[1024,128]{0,1:T(8,128)S(1)} %add.111), channel_id=1, source_target_pairs={{0,2},{1,3},{2,0},{3,1},{4,6},{5,7},{6,4},{7,5},{8,10},{9,11},{10,... | collective-permute-start | bytes 1572872 | tf_op jit(solution)/shard_map/while/body/eval_jaxpr/ppermute | solution.py:57
  228.2 14.7 %collective-permute-start.2 = (f32[1024,128]{0,1:T(8,128)S(1)}, f32[1024,128]{0,1:T(8,128)S(1)}, u32[]{:S(2)}, u32[]{:S(2)}) collective-permute-start(f32[1024,128]{0,1:T(8,128)S(1)} %add.112), channel_id=1, source_target_pairs={{0,4},{1,5},{2,6},{3,7},{4,0},{5,1},{6,2},{7,3},{8,12},{9,13},{10,... | collective-permute-start | bytes 1572872 | tf_op jit(solution)/shard_map/while/body/eval_jaxpr/ppermute | solution.py:57
  280.8 14.1 %collective-permute-start.1 = (f32[1024,128]{0,1:T(8,128)S(1)}, f32[1024,128]{0,1:T(8,128)S(1)}, u32[]{:S(2)}, u32[]{:S(2)}) collective-permute-start(f32[1024,128]{0,1:T(8,128)S(1)} %add.111), channel_id=1, source_target_pairs={{0,2},{1,3},{2,0},{3,1},{4,6},{5,7},{6,4},{7,5},{8,10},{9,11},{10,... | collective-permute-start | bytes 1572872 | tf_op jit(solution)/shard_map/while/body/eval_jaxpr/ppermute | solution.py:57
  294.9 14.7 %collective-permute-start.2 = (f32[1024,128]{0,1:T(8,128)S(1)}, f32[1024,128]{0,1:T(8,128)S(1)}, u32[]{:S(2)}, u32[]{:S(2)}) collective-permute-start(f32[1024,128]{0,1:T(8,128)S(1)} %add.112), channel_id=1, source_target_pairs={{0,4},{1,5},{2,6},{3,7},{4,0},{5,1},{6,2},{7,3},{8,12},{9,13},{10,... | collective-permute-start | bytes 1572872 | tf_op jit(solution)/shard_map/while/body/eval_jaxpr/ppermute | solution.py:57
  362.4 14.7 %collective-permute-start.2 = (f32[1024,128]{0,1:T(8,128)S(1)}, f32[1024,128]{0,1:T(8,128)S(1)}, u32[]{:S(2)}, u32[]{:S(2)}) collective-permute-start(f32[1024,128]{0,1:T(8,128)S(1)} %add.112), channel_id=1, source_target_pairs={{0,4},{1,5},{2,6},{3,7},{4,0},{5,1},{6,2},{7,3},{8,12},{9,13},{10,... | collective-permute-start | bytes 1572872 | tf_op jit(solution)/shard_map/while/body/eval_jaxpr/ppermute | solution.py:57
  416.1 14.1 %collective-permute-start.1 = (f32[1024,128]{0,1:T(8,128)S(1)}, f32[1024,128]{0,1:T(8,128)S(1)}, u32[]{:S(2)}, u32[]{:S(2)}) collective-permute-start(f32[1024,128]{0,1:T(8,128)S(1)} %add.111), channel_id=1, source_target_pairs={{0,2},{1,3},{2,0},{3,1},{4,6},{5,7},{6,4},{7,5},{8,10},{9,11},{10,... | collective-permute-start | bytes 1572872 | tf_op jit(solution)/shard_map/while/body/eval_jaxpr/ppermute | solution.py:57
  430.2 14.7 %collective-permute-start.2 = (f32[1024,128]{0,1:T(8,128)S(1)}, f32[1024,128]{0,1:T(8,128)S(1)}, u32[]{:S(2)}, u32[]{:S(2)}) collective-permute-start(f32[1024,128]{0,1:T(8,128)S(1)} %add.112), channel_id=1, source_target_pairs={{0,4},{1,5},{2,6},{3,7},{4,0},{5,1},{6,2},{7,3},{8,12},{9,13},{10,... | collective-permute-start | bytes 1572872 | tf_op jit(solution)/shard_map/while/body/eval_jaxpr/ppermute | solution.py:57
  498.1 14.7 %collective-permute-start.2 = (f32[1024,128]{0,1:T(8,128)S(1)}, f32[1024,128]{0,1:T(8,128)S(1)}, u32[]{:S(2)}, u32[]{:S(2)}) collective-permute-start(f32[1024,128]{0,1:T(8,128)S(1)} %add.112), channel_id=1, source_target_pairs={{0,4},{1,5},{2,6},{3,7},{4,0},{5,1},{6,2},{7,3},{8,12},{9,13},{10,... | collective-permute-start | bytes 1572872 | tf_op jit(solution)/shard_map/while/body/eval_jaxpr/ppermute | solution.py:57
  565.9 14.7 %collective-permute-start.2 = (f32[1024,128]{0,1:T(8,128)S(1)}, f32[1024,128]{0,1:T(8,128)S(1)}, u32[]{:S(2)}, u32[]{:S(2)}) collective-permute-start(f32[1024,128]{0,1:T(8,128)S(1)} %add.112), channel_id=1, source_target_pairs={{0,4},{1,5},{2,6},{3,7},{4,0},{5,1},{6,2},{7,3},{8,12},{9,13},{10,... | collective-permute-start | bytes 1572872 | tf_op jit(solution)/shard_map/while/body/eval_jaxpr/ppermute | solution.py:57
  633.7 14.7 %collective-permute-start.2 = (f32[1024,128]{0,1:T(8,128)S(1)}, f32[1024,128]{0,1:T(8,128)S(1)}, u32[]{:S(2)}, u32[]{:S(2)}) collective-permute-start(f32[1024,128]{0,1:T(8,128)S(1)} %add.112), channel_id=1, source_target_pairs={{0,4},{1,5},{2,6},{3,7},{4,0},{5,1},{6,2},{7,3},{8,12},{9,13},{10,... | collective-permute-start | bytes 1572872 | tf_op jit(solution)/shard_map/while/body/eval_jaxpr/ppermute | solution.py:57
  687.5 14.1 %collective-permute-start.1 = (f32[1024,128]{0,1:T(8,128)S(1)}, f32[1024,128]{0,1:T(8,128)S(1)}, u32[]{:S(2)}, u32[]{:S(2)}) collective-permute-start(f32[1024,128]{0,1:T(8,128)S(1)} %add.111), channel_id=1, source_target_pairs={{0,2},{1,3},{2,0},{3,1},{4,6},{5,7},{6,4},{7,5},{8,10},{9,11},{10,... | collective-permute-start | bytes 1572872 | tf_op jit(solution)/shard_map/while/body/eval_jaxpr/ppermute | solution.py:57
  701.6 14.7 %collective-permute-start.2 = (f32[1024,128]{0,1:T(8,128)S(1)}, f32[1024,128]{0,1:T(8,128)S(1)}, u32[]{:S(2)}, u32[]{:S(2)}) collective-permute-start(f32[1024,128]{0,1:T(8,128)S(1)} %add.112), channel_id=1, source_target_pairs={{0,4},{1,5},{2,6},{3,7},{4,0},{5,1},{6,2},{7,3},{8,12},{9,13},{10,... | collective-permute-start | bytes 1572872 | tf_op jit(solution)/shard_map/while/body/eval_jaxpr/ppermute | solution.py:57
  755.3 14.1 %collective-permute-start.1 = (f32[1024,128]{0,1:T(8,128)S(1)}, f32[1024,128]{0,1:T(8,128)S(1)}, u32[]{:S(2)}, u32[]{:S(2)}) collective-permute-start(f32[1024,128]{0,1:T(8,128)S(1)} %add.111), channel_id=1, source_target_pairs={{0,2},{1,3},{2,0},{3,1},{4,6},{5,7},{6,4},{7,5},{8,10},{9,11},{10,... | collective-permute-start | bytes 1572872 | tf_op jit(solution)/shard_map/while/body/eval_jaxpr/ppermute | solution.py:57
  769.4 14.7 %collective-permute-start.2 = (f32[1024,128]{0,1:T(8,128)S(1)}, f32[1024,128]{0,1:T(8,128)S(1)}, u32[]{:S(2)}, u32[]{:S(2)}) collective-permute-start(f32[1024,128]{0,1:T(8,128)S(1)} %add.112), channel_id=1, source_target_pairs={{0,4},{1,5},{2,6},{3,7},{4,0},{5,1},{6,2},{7,3},{8,12},{9,13},{10,... | collective-permute-start | bytes 1572872 | tf_op jit(solution)/shard_map/while/body/eval_jaxpr/ppermute | solution.py:57
  837.3 14.7 %collective-permute-start.2 = (f32[1024,128]{0,1:T(8,128)S(1)}, f32[1024,128]{0,1:T(8,128)S(1)}, u32[]{:S(2)}, u32[]{:S(2)}) collective-permute-start(f32[1024,128]{0,1:T(8,128)S(1)} %add.112), channel_id=1, source_target_pairs={{0,4},{1,5},{2,6},{3,7},{4,0},{5,1},{6,2},{7,3},{8,12},{9,13},{10,... | collective-permute-start | bytes 1572872 | tf_op jit(solution)/shard_map/while/body/eval_jaxpr/ppermute | solution.py:57
  905.2 14.7 %collective-permute-start.2 = (f32[1024,128]{0,1:T(8,128)S(1)}, f32[1024,128]{0,1:T(8,128)S(1)}, u32[]{:S(2)}, u32[]{:S(2)}) collective-permute-start(f32[1024,128]{0,1:T(8,128)S(1)} %add.112), channel_id=1, source_target_pairs={{0,4},{1,5},{2,6},{3,7},{4,0},{5,1},{6,2},{7,3},{8,12},{9,13},{10,... | collective-permute-start | bytes 1572872 | tf_op jit(solution)/shard_map/while/body/eval_jaxpr/ppermute | solution.py:57
  973.0 14.7 %collective-permute-start.2 = (f32[1024,128]{0,1:T(8,128)S(1)}, f32[1024,128]{0,1:T(8,128)S(1)}, u32[]{:S(2)}, u32[]{:S(2)}) collective-permute-start(f32[1024,128]{0,1:T(8,128)S(1)} %add.112), channel_id=1, source_target_pairs={{0,4},{1,5},{2,6},{3,7},{4,0},{5,1},{6,2},{7,3},{8,12},{9,13},{10,... | collective-permute-start | bytes 1572872 | tf_op jit(solution)/shard_map/while/body/eval_jaxpr/ppermute | solution.py:57
  (85 other events, 813.7 us)
Sparse Core Ops, SparseCore 0:
  1028.1 50.1 reduce-scatter.1
